TPU v7x, 32 devices: a whole 2x2x4 slice. The times are simulated.
32 devices in a mesh: rep: 2 (over y), grp: 4 (over z), sub: 4 (over x, core).
Axes of the slice: x: 2, y: 2, z: 4, core: 2. Of those that a mesh axis runs over, the one named last changes fastest.
Arguments:
- embeddings: bfloat16 [8192, 1024], P(('rep', 'grp', 'sub')), parts along dimension 0, may hold values from -6 to 6
- cluster_ids: int32 [8192, 1], P(('rep', 'grp', 'sub')), parts along dimension 0, may hold values from 0 to 3; in each aligned block of 256 rows (0 to 255, 256 to 511, ...) at most 128 rows name the same one
Outputs:
- max_similarity: float32 [8192], P(('rep', 'grp', 'sub')), parts along dimension 0
There are 2 independent parts, one for each index of `rep`. A program takes and returns all parts, laid end to end along the dimension named above; each array names one. Nothing has to cross between parts.
Inputs may be any that keep to these rules, and one draw needn't show every extreme that they name: `cluster_ids`: cluster numbers run from 0 to 3; among the rows of one device no cluster is named by more than 128 rows, and in every draw some cluster is named by exactly 128 rows of some device.
All inputs are finite; a program needn't handle non-finite values.
Results may differ from a plain program's by a relative error of at most 0.0014.
Values may be sent and summed in bfloat16 or wider, within the bound.
A program may use at most 64 MiB of HBM per device.

v0:
```python
import math

import jax
import jax.numpy as jnp
from jax import lax
from jax.sharding import PartitionSpec as P


def from_behind(value, axis, by):
    peers = lax.axis_size(axis)
    return lax.ppermute(value, axis, [(i, (i + by) % peers) for i in range(peers)])


def masked_maxima(left_rows, right_rows, right_present, excluded):
    similar = jnp.dot(left_rows, right_rows.T, preferred_element_type=jnp.float32)
    allowed = (right_present[None, :] > 0) & jnp.logical_not(excluded)
    return jnp.where(allowed, similar, jnp.float32(-1.0))


def local(embeddings, cluster_ids):
    rows_dev, features = embeddings.shape
    groups = lax.axis_size("grp")
    subgroup = lax.axis_size("sub")
    capacity = 2 * rows_dev // groups
    floats = embeddings.astype(jnp.float32)
    unit_rows = (
        floats
        * lax.rsqrt(jnp.mean(floats * floats, axis=1, keepdims=True) + 1e-06)
        / math.sqrt(features)
    ).astype(jnp.bfloat16)
    labels = cluster_ids[:, 0]
    member_table = (labels[:, None] == jnp.arange(groups, dtype=jnp.int32)[None, :]).astype(
        jnp.int32
    )
    running = jnp.cumsum(member_table, axis=0)
    within = jnp.sum(jnp.where(member_table > 0, running - 1, 0), axis=1)
    slot_index = labels * capacity + within
    outgoing = jnp.zeros((groups * capacity, features), jnp.bfloat16).at[slot_index].set(unit_rows)
    occupied = jnp.zeros((groups * capacity,), jnp.int32).at[slot_index].set(1)
    arrived, arrived_present = (
        lax.all_to_all(
            outgoing.reshape(groups, capacity, features),
            "grp",
            split_axis=0,
            concat_axis=0,
            tiled=True,
        ),
        lax.all_to_all(
            occupied.reshape(groups, capacity), "grp", split_axis=0, concat_axis=0, tiled=True
        ),
    )
    owned_rows = arrived.reshape(groups * capacity, features)
    present = arrived_present.reshape(groups * capacity)
    held = owned_rows.shape[0]
    positions = jnp.arange(held, dtype=jnp.int32)
    excluded = positions[:, None] == positions[None, :]
    highest = jnp.max(masked_maxima(owned_rows, owned_rows, present, excluded), axis=1)
    no_exclusion = jnp.zeros((held, held), dtype=bool)
    for offset in range(1, subgroup // 2 + 1):
        peer_rows, peer_present = from_behind((owned_rows, present), "sub", offset)
        scores = masked_maxima(owned_rows, peer_rows, peer_present, no_exclusion)
        highest = jnp.maximum(highest, jnp.max(scores, axis=1))
        if 2 * offset != subgroup:
            column_best = jnp.max(
                jnp.where(present[:, None] > 0, scores, jnp.float32(-1.0)), axis=0
            )
            returned_best = from_behind(column_best, "sub", -offset)
            highest = jnp.maximum(highest, returned_best)
    returned = lax.all_to_all(
        highest.reshape(groups, capacity), "grp", split_axis=0, concat_axis=0, tiled=True
    )
    return returned.reshape(groups * capacity)[slot_index]


def solution(mesh):
    return jax.shard_map(
        local,
        mesh=mesh,
        in_specs=(P(("rep", "grp", "sub"), None), P(("rep", "grp", "sub"), None)),
        out_specs=P(("rep", "grp", "sub")),
        check_vma=False,
    )
```

profile of v0, /device:TPU:0, one launch (start us, length us, event | category | flops | bytes accessed | tf_op | source)
XLA Modules:
  0.0 86.8 jit_solution(2661615473849376963)
XLA Ops:
  0.0 0.0 copy-start.1
  0.0 0.0 copy-start
  0.0 0.7 copy-done.1
  0.7 1.2 %reduce-window.6 = s32[4,2,128]{2,1,0:T(2,128)S(1)} reduce-window(s32[4,2,128]{2,1,0:T(2,128)S(1)} %compare_convert_fusion, s32[]{:T(128)} %constant.12.clone.1), window={size=1x1x128 pad=0_0x0_0x127_0}, to_apply=%region_0.0 | reduce-window | flops 130048 | bytes 8196 | tf_op jit(solution)/shard_map/reduce-window
  1.9 0.1 slice.10
  2.0 0.1 copy.6
  2.1 0.1 copy.7
  2.2 0.1 add_bitcast_fusion
  2.3 1.2 %fusion.1 = f32[256]{0:T(256)S(1)} fusion(bf16[256,1024]{1,0:T(8,128)(2,1)} %param.2), kind=kLoop, calls=%fused_computation.7 | loop fusion | flops 786176 | bytes 525312 | tf_op jit(solution)/shard_map/reduce_sum | solution.py:28
  3.6 0.0 copy-done
  3.6 2.0 %scatter_custom_fusion.1 = bf16[512,1024]{1,0:T(8,128)(2,1)S(1)} fusion(s32[256]{0:T(256)S(1)} %bitcast.44, bf16[256,1024]{1,0:T(8,128)(2,1)S(1)} %copy-done, f32[]{:T(128)} %constant.8.clone.1, f32[256]{0:T(256)S(1)} %add_rsqrt_fusion, bf16[]{:T(256)} %constant.17.clone.1), kind=kCustom, calls=%fused_computation.16 | custom fusion | flops 1048576 | bytes 1573894 | tf_op jit(solution)/shard_map/scatter | solution.py:38
  5.6 31.9 %all_to_all.23 = bf16[4,128,1024]{2,1,0:T(8,128)(2,1)S(1)} all-to-all(bf16[4,128,1024]{2,1,0:T(8,128)(2,1)S(1)} %bitcast.32), channel_id=1, replica_groups=mesh['rep'=2,'grp'=4,'sub'=4] {'grp'}, dimensions={0} | all-to-all | bytes 2097152 | tf_op jit(solution)/shard_map/all_to_all | solution.py:41
  37.5 0.0 collective-permute-start.1
  37.5 1.4 %scatter_custom_fusion = s32[512]{0:T(512)S(1)} fusion(s32[256]{0:T(256)S(1)} %bitcast.45, s32[256]{0:T(256)S(1)} %broadcast.58, s32[]{:T(128)} %constant.12.clone.1), kind=kCustom, calls=%fused_computation.34 | custom fusion | bytes 2052 | tf_op jit(solution)/shard_map/scatter | solution.py:39
  38.9 8.1 %all_to_all.24 = s32[4,1,128]{2,1,0:T(1,128)S(1)} all-to-all(s32[4,1,128]{2,1,0:T(1,128)S(1)} %bitcast.43), channel_id=1, replica_groups=mesh['rep'=2,'grp'=4,'sub'=4] {'grp'}, dimensions={0} | all-to-all | bytes 4096 | tf_op jit(solution)/shard_map/all_to_all | solution.py:48
  47.0 1.5 %collective-permute-start.3 = (s32[512]{0:T(512)S(1)}, s32[512]{0:T(512)S(1)}, u32[]{:S(2)}, u32[]{:S(2)}) collective-permute-start(s32[512]{0:T(512)S(1)} %bitcast.40), channel_id=1, source_target_pairs={{0,2},{1,3},{2,0},{3,1},{4,6},{5,7},{6,4},{7,5},{8,10},{9,11},{10,... | collective-permute-start | bytes 6152 | tf_op jit(solution)/shard_map/ppermute | solution.py:11
  48.5 0.0 collective-permute-start
  48.5 0.5 collective-permute-start.4
  49.0 1.6 %collective-permute-done.3 = s32[512]{0:T(512)S(1)} collective-permute-done((s32[512]{0:T(512)S(1)}, s32[512]{0:T(512)S(1)}, u32[]{:S(2)}, u32[]{:S(2)}) %collective-permute-start.3) | collective-permute-done | bytes 2080 | tf_op jit(solution)/shard_map/ppermute | solution.py:11
  50.6 1.2 %collective-permute-done = s32[512]{0:T(512)S(1)} collective-permute-done((s32[512]{0:T(512)S(1)}, s32[512]{0:T(512)S(1)}, u32[]{:S(2)}, u32[]{:S(2)}) %collective-permute-start) | collective-permute-done | bytes 2080 | tf_op jit(solution)/shard_map/ppermute | solution.py:11
  51.8 0.8 fusion
  52.5 0.0 collective-permute-done.1
  52.5 0.9 %select_reduce_fusion.2 = (f32[512]{0:T(512)S(1)}, f32[512]{0:T(512)S(1)}) fusion(pred[512]{0:T(512)(128)(4,1)S(1)} %broadcast_compare_fusion.1, pred[512]{0:T(512)(128)(4,1)S(1)} %broadcast_compare_fusion.2, bf16[512,1024]{1,0:T(8,128)(2,1)S(1)} %bitcast.36, bf16[512,1024]{1,0:T(8,128)(2,1)S(1)} %collective-permute-done.1), kind=kOutput, calls=%fused_computation.15 | convolution fusion | flops 537918464 | bytes 2102272 | tf_op jit(solution)/shard_map/dot_general | solution.py:15
  53.4 1.9 %collective-permute-start.2 = (f32[512]{0:T(512)S(1)}, f32[512]{0:T(512)S(1)}, u32[]{:S(2)}, u32[]{:S(2)}) collective-permute-start(f32[512]{0:T(512)S(1)} %get-tuple-element.6), channel_id=1, source_target_pairs={{0,3},{1,0},{2,1},{3,2},{4,7},{5,4},{6,5},{7,6},{8,11},{9,8},{10,9... | collective-permute-start | bytes 6152 | tf_op jit(solution)/shard_map/ppermute | solution.py:11
  55.3 18.9 %collective-permute-done.4 = bf16[512,1024]{1,0:T(8,128)(2,1)S(1)} collective-permute-done((bf16[512,1024]{1,0:T(8,128)(2,1)S(1)}, bf16[512,1024]{1,0:T(8,128)(2,1)S(1)}, u32[]{:S(2)}, u32[]{:S(2)}) %collective-permute-start.4) | collective-permute-done | bytes 1048608 | tf_op jit(solution)/shard_map/ppermute | solution.py:11
  74.2 0.8 select_reduce_fusion
  75.0 0.0 collective-permute-done.2
  75.0 0.6 maximum_maximum_fusion
  75.6 3.2 %all-to-all-start.2 = ((f32[4,1,128]{2,1,0:T(1,128)}), f32[4,1,128]{2,1,0:T(1,128)S(1)}, u32[]{:S(2)}, u32[]{:S(2)}) async-start(f32[4,1,128]{2,1,0:T(1,128)} %bitcast.10), calls=%async_computation.2 | async-start | bytes 4096 | tf_op jit(solution)/shard_map/all_to_all | solution.py:69
  78.9 5.4 %all-to-all-done.2 = f32[4,1,128]{2,1,0:T(1,128)S(1)} async-done(((f32[4,1,128]{2,1,0:T(1,128)}), f32[4,1,128]{2,1,0:T(1,128)S(1)}, u32[]{:S(2)}, u32[]{:S(2)}) %all-to-all-start.2) | async-done | bytes 2080 | tf_op jit(solution)/shard_map/all_to_all | solution.py:69
  84.3 2.5 %gather_fusion = f32[256]{0:T(256)} fusion(f32[512]{0:T(512)S(1)} %bitcast.31, s32[1024]{0:T(1024)S(1)} %pad_clamp_fusion), kind=kCustom, calls=%fused_computation | custom fusion | bytes 3072 | tf_op jit(solution)/shard_map/gather | solution.py:72
  (11 shorter events, 0.1 us)
Async XLA Ops:
  0.0 0.7 copy-start.1
  0.0 3.6 %copy-start = (bf16[256,1024]{1,0:T(8,128)(2,1)S(1)}, bf16[256,1024]{1,0:T(8,128)(2,1)}, u32[]{:S(2)}) copy-start(bf16[256,1024]{1,0:T(8,128)(2,1)} %param.2) | copy-start | bytes 1572868
  37.5 15.1 %collective-permute-start.1 = (bf16[512,1024]{1,0:T(8,128)(2,1)S(1)}, bf16[512,1024]{1,0:T(8,128)(2,1)S(1)}, u32[]{:S(2)}, u32[]{:S(2)}) collective-permute-start(bf16[512,1024]{1,0:T(8,128)(2,1)S(1)} %bitcast.33), channel_id=1, source_target_pairs={{0,1},{1,2},{2,3},{3,0},{4,5},{5,6},{6,7},{7,4},{8,9},{9,10},{10,1... | collective-permute-start | bytes 3145736 | tf_op jit(solution)/shard_map/ppermute | solution.py:11
  47.0 3.6 %collective-permute-start.3 = (s32[512]{0:T(512)S(1)}, s32[512]{0:T(512)S(1)}, u32[]{:S(2)}, u32[]{:S(2)}) collective-permute-start(s32[512]{0:T(512)S(1)} %bitcast.40), channel_id=1, source_target_pairs={{0,2},{1,3},{2,0},{3,1},{4,6},{5,7},{6,4},{7,5},{8,10},{9,11},{10,... | collective-permute-start | bytes 6152 | tf_op jit(solution)/shard_map/ppermute | solution.py:11
  48.5 3.3 %collective-permute-start = (s32[512]{0:T(512)S(1)}, s32[512]{0:T(512)S(1)}, u32[]{:S(2)}, u32[]{:S(2)}) collective-permute-start(s32[512]{0:T(512)S(1)} %bitcast.41), channel_id=1, source_target_pairs={{0,1},{1,2},{2,3},{3,0},{4,5},{5,6},{6,7},{7,4},{8,9},{9,10},{10,1... | collective-permute-start | bytes 6152 | tf_op jit(solution)/shard_map/ppermute | solution.py:11
  48.5 25.8 %collective-permute-start.4 = (bf16[512,1024]{1,0:T(8,128)(2,1)S(1)}, bf16[512,1024]{1,0:T(8,128)(2,1)S(1)}, u32[]{:S(2)}, u32[]{:S(2)}) collective-permute-start(bf16[512,1024]{1,0:T(8,128)(2,1)S(1)} %bitcast.34), channel_id=1, source_target_pairs={{0,2},{1,3},{2,0},{3,1},{4,6},{5,7},{6,4},{7,5},{8,10},{9,11},{10,... | collective-permute-start | bytes 3145736 | tf_op jit(solution)/shard_map/ppermute | solution.py:11
  53.4 21.6 %collective-permute-start.2 = (f32[512]{0:T(512)S(1)}, f32[512]{0:T(512)S(1)}, u32[]{:S(2)}, u32[]{:S(2)}) collective-permute-start(f32[512]{0:T(512)S(1)} %get-tuple-element.6), channel_id=1, source_target_pairs={{0,3},{1,0},{2,1},{3,2},{4,7},{5,4},{6,5},{7,6},{8,11},{9,8},{10,9... | collective-permute-start | bytes 6152 | tf_op jit(solution)/shard_map/ppermute | solution.py:11
  75.6 8.6 %all-to-all-start.2 = ((f32[4,1,128]{2,1,0:T(1,128)}), f32[4,1,128]{2,1,0:T(1,128)S(1)}, u32[]{:S(2)}, u32[]{:S(2)}) async-start(f32[4,1,128]{2,1,0:T(1,128)} %bitcast.10), calls=%async_computation.2 | async-start | bytes 4096 | tf_op jit(solution)/shard_map/all_to_all | solution.py:69
where the time goes:
time: 87.1 us; the launch traced here: 86.8 us
  blocking collectives  40 us (46%)
  waiting for transfers between devices  27 us (31%)
  starting transfers between devices  7.18 us (8%)
  other arithmetic  5.22 us (6%)
  local copies, waits for them, and re-layouts  4.86 us (6%)
  matrix products  2.44 us (3%)
    all_to_all x1, blocking collectives, local(): lax.all_to_all(outgoing.reshape(groups, capacity, features), 'grp', split...  31.9 us
    ppermute x5, waiting for transfers between devices, from_behind(): lax.ppermute(value, axis, [(i, (i + by) % peers) for i in range(peers)])  21.6 us
    all_to_all x1, blocking collectives, local(): lax.all_to_all(occupied.reshape(groups, capacity), 'grp', split_axis=0, c...  8.11 us
    all_to_all x1, waiting for transfers between devices, local(): lax.all_to_all(highest.reshape(groups, capacity), 'grp', split_axis=0, co...  5.37 us
    ppermute x5, starting transfers between devices, from_behind(): lax.ppermute(value, axis, [(i, (i + by) % peers) for i in range(peers)])  3.93 us
    all_to_all x1, starting transfers between devices, local(): lax.all_to_all(highest.reshape(groups, capacity), 'grp', split_axis=0, co...  3.24 us
    gather x1, local copies, waits for them, and re-layouts, local(): return returned.reshape(groups * capacity)[slot_index]  2.5 us
    dot_general x3, matrix products, masked_maxima(): jnp.dot(left_rows, right_rows.T, preferred_element_type=jnp.float32)  2.44 us
  transfers between devices with their start and end apart: 6, of which 4 were waited for; matrix products, arithmetic and copies ran while one was open for 4% of the time, Pallas kernels for 0%

commit v1 on v0

--- a/solution.py
+++ b/solution.py
@@ -1,9 +1,17 @@
+import functools
 import math
 
 import jax
 import jax.numpy as jnp
 from jax import lax
+from jax.experimental import pallas as pl
+from jax.experimental.pallas import tpu as pltpu
 from jax.sharding import PartitionSpec as P
+
+LANES = 128
+SUBLANES = 8
+VMEM_BUDGET = 24 << 20
+MESH = pl.DeviceIdType.MESH
 
 
 def from_behind(value, axis, by):
@@ -17,17 +25,21 @@
     return jnp.where(allowed, similar, jnp.float32(-1.0))
 
 
-def local(embeddings, cluster_ids):
+def unit_of(rows, features):
+    floats = rows.astype(jnp.float32)
+    return (
+        floats
+        * lax.rsqrt(jnp.mean(floats * floats, axis=1, keepdims=True) + 1e-06)
+        / math.sqrt(features)
+    ).astype(jnp.bfloat16)
+
+
+def by_owner(embeddings, cluster_ids):
     rows_dev, features = embeddings.shape
     groups = lax.axis_size("grp")
     subgroup = lax.axis_size("sub")
     capacity = 2 * rows_dev // groups
-    floats = embeddings.astype(jnp.float32)
-    unit_rows = (
-        floats
-        * lax.rsqrt(jnp.mean(floats * floats, axis=1, keepdims=True) + 1e-06)
-        / math.sqrt(features)
-    ).astype(jnp.bfloat16)
+    unit_rows = unit_of(embeddings, features)
     labels = cluster_ids[:, 0]
     member_table = (labels[:, None] == jnp.arange(groups, dtype=jnp.int32)[None, :]).astype(
         jnp.int32
@@ -72,6 +84,287 @@
     return returned.reshape(groups * capacity)[slot_index]
 
 
+def meet_kernel(
+    groups, subgroup, chunks,
+    emb_ref, ids_ref, out_ref,
+    level, foreign, lane_ids, level_ids, ids_col, row_part, col_part,
+    ret_out, ret_in, col_out, col_in,
+    ids_send, ids_recv, lid_send, lid_recv, lvl_send, lvl_recv, fwd_send,
+    z_send, z_recv, ret_send, ret_recv, col_send, col_recv,
+):
+    rows, features = emb_ref.shape
+    size = rows // chunks
+    pivot = groups // 2
+    z = lax.axis_index("grp")
+    s = lax.axis_index("sub")
+    partner = s + 1 - 2 * lax.rem(s, 2)
+    others = subgroup // 2
+
+    def peer(k):
+        return lax.rem(s + k, subgroup)
+
+    def lane(k):
+        return lax.rem(z + k, groups)
+
+    barrier = pltpu.get_barrier_semaphore()
+    for k in range(1, subgroup):
+        pl.semaphore_signal(barrier, 1, device_id={"sub": peer(k)}, device_id_type=MESH)
+    for k in range(1, groups):
+        pl.semaphore_signal(barrier, 1, device_id={"grp": lane(k)}, device_id_type=MESH)
+
+    def slot(b):
+        return pl.ds(pl.multiple_of(b * rows, rows), rows)
+
+    def piece(b, k):
+        return pl.ds(pl.multiple_of(b * rows + k * size, size), size)
+
+    def part(k):
+        return pl.ds(pl.multiple_of(k * size, size), size)
+
+    def normalize(k, carry):
+        level[piece(s, k), :] = unit_of(emb_ref[part(k), :], features)
+        return carry
+
+    lax.fori_loop(0, chunks, normalize, 0)
+    level_ids[s] = ids_ref[...]
+    lane_ids[z] = ids_ref[...]
+    col_part[...] = jnp.full(col_part.shape, -1.0, jnp.float32)
+    pl.semaphore_wait(barrier, subgroup + groups - 2)
+
+    def remote(src, dst, send, recv, where):
+        return pltpu.make_async_remote_copy(
+            src_ref=src, dst_ref=dst, send_sem=send, recv_sem=recv,
+            device_id=where, device_id_type=MESH,
+        )
+
+    def level_ids_copy(k, owner):
+        return remote(ids_ref, level_ids.at[owner], lid_send.at[k], lid_recv.at[owner], {"sub": peer(k)})
+
+    def lane_ids_copy(k, owner):
+        return remote(ids_ref, lane_ids.at[owner], ids_send.at[k], ids_recv.at[owner], {"grp": lane(k)})
+
+    def own_to_lane(k, where):
+        return remote(
+            level.at[piece(s, k), :], foreign.at[z, part(k), :], z_send.at[z, k], z_recv.at[z, k],
+            {"grp": where},
+        )
+
+    def passed_on(i, k, where):
+        block = foreign.at[i, part(k), :]
+        return remote(block, block, z_send.at[i, k], z_recv.at[i, k], {"grp": where})
+
+    def block_to_peer(owner, send, where):
+        block = level.at[slot(owner), :]
+        return remote(block, block, send, lvl_recv.at[owner], {"sub": where})
+
+    for k in range(1, groups):
+        lane_ids_copy(k, z).start()
+    for k in range(1, subgroup):
+        level_ids_copy(k, s).start()
+
+    sends_right = z < pivot
+    sends_left = z > pivot
+
+    @pl.when(sends_right)
+    def _():
+        lax.fori_loop(0, chunks, lambda k, c: (own_to_lane(k, z + 1).start(), c)[1], 0)
+
+    @pl.when(sends_left)
+    def _():
+        lax.fori_loop(0, chunks, lambda k, c: (own_to_lane(k, z - 1).start(), c)[1], 0)
+
+    for k in range(1, others):
+        block_to_peer(s, lvl_send.at[k], peer(2 * k)).start()
+    block_to_peer(s, lvl_send.at[0], partner).start()
+
+    def visits(i):
+        return z > i if i < pivot else (z >= pivot) & (z < i)
+
+    def passes(i):
+        return (z > i) & (z < groups - 1) if i < pivot else (z > pivot) & (z < i)
+
+    def onward(i):
+        return z + 1 if i < pivot else z - 1
+
+    def take(i, k):
+        passed_on(i, k, z).wait_recv()
+
+        @pl.when(passes(i))
+        def _():
+            passed_on(i, k, onward(i)).start()
+
+    early = list(range(pivot - 1, 0, -1)) + list(range(pivot + 1, groups))
+    for i in early + [0]:
+        @pl.when(visits(i) if i else z == 1)
+        def _(i=i):
+            lax.fori_loop(0, chunks, lambda k, c: (take(i, k), c)[1], 0)
+
+    for k in range(1, others):
+        came_from = peer(2 * k)
+        block_to_peer(came_from, lvl_send.at[0], s).wait_recv()
+        block_to_peer(came_from, fwd_send.at[k], partner).start()
+    for k in range(0, others):
+        came_from = lax.rem(partner + 2 * k, subgroup)
+        block_to_peer(came_from, lvl_send.at[0], s).wait_recv()
+
+    for k in range(1, groups):
+        lane_ids_copy(k, lane(k)).wait_recv()
+    for k in range(1, subgroup):
+        level_ids_copy(k, peer(k)).wait_recv()
+    for i in range(groups):
+        ids_col[i] = jnp.broadcast_to(lane_ids[i], (LANES, rows)).T
+
+    width = subgroup * rows
+
+    def meet(lines, own_ids, shift, store_row, keep_columns):
+        similar = lax.dot_general(
+            lines, level[...], (((1,), (1,)), ((), ())), preferred_element_type=jnp.float32
+        )
+        best = jnp.full((size, LANES), -1.0, jnp.float32)
+        for at in range(0, width, LANES):
+            ids_at = level_ids[at // rows, :, at % rows : at % rows + LANES]
+            same = own_ids == ids_at
+            if shift is not None:
+                across = lax.broadcasted_iota(jnp.int32, (size, LANES), 1) + at
+                down = lax.broadcasted_iota(jnp.int32, (size, LANES), 0) + shift
+                same = same & (across != down)
+            kept = jnp.where(same, similar[:, at : at + LANES], jnp.float32(-1.0))
+            best = jnp.maximum(best, kept)
+            if keep_columns:
+                columns = jnp.max(kept.reshape(size // SUBLANES, SUBLANES, LANES), axis=0)
+                col_part[:, at : at + LANES] = jnp.maximum(col_part[:, at : at + LANES], columns)
+        store_row(best)
+
+    def meet_foreign(i, k):
+        def store(best):
+            row_part[i, part(k), :] = best
+
+        meet(foreign[i, part(k), :], ids_col[i, part(k), :], None, store, True)
+
+    def step(k, carry):
+        def store(best):
+            row_part[z, part(k), :] = best
+
+        meet(level[piece(s, k), :], ids_col[z, part(k), :], s * rows + k * size, store, False)
+        for i in early:
+            @pl.when(visits(i))
+            def _(i=i):
+                meet_foreign(i, k)
+
+        @pl.when(z > 1)
+        def _():
+            take(0, k)
+
+        @pl.when(z > 0)
+        def _():
+            meet_foreign(0, k)
+
+        return carry
+
+    lax.fori_loop(0, chunks, step, 0)
+
+    def flat(i):
+        return jnp.max(row_part[i].T, axis=0, keepdims=True)
+
+    def ret_copy(i, owner, where):
+        return remote(ret_out.at[i], ret_in.at[owner], ret_send.at[i], ret_recv.at[owner], {"grp": where})
+
+    def col_copy(k, owner):
+        return remote(col_out.at[peer(k)], col_in.at[owner], col_send.at[k], col_recv.at[owner], {"sub": peer(k)})
+
+    for i in [0] + early:
+        @pl.when(visits(i))
+        def _(i=i):
+            ret_out[i] = flat(i)
+
+    for b in range(subgroup):
+        col_out[b] = jnp.max(col_part[:, b * rows : (b + 1) * rows], axis=0, keepdims=True)
+    for i in [0] + early:
+        @pl.when(visits(i))
+        def _(i=i):
+            ret_copy(i, z, i).start()
+    for k in range(1, subgroup):
+        col_copy(k, s).start()
+
+    out_ref[...] = jnp.maximum(flat(z), col_out[s])
+    for k in range(1, subgroup):
+        col_copy(k, peer(k)).wait_recv()
+        out_ref[...] = jnp.maximum(out_ref[...], col_in[peer(k)])
+    for j in range(1, groups):
+        @pl.when((z < j) & (z < pivot) | (z > j) & (z > pivot) & (j >= pivot))
+        def _(j=j):
+            ret_copy(0, j, z).wait_recv()
+            out_ref[...] = jnp.maximum(out_ref[...], ret_in[j])
+
+    for k in range(1, groups):
+        lane_ids_copy(k, z).wait_send()
+    for k in range(1, subgroup):
+        level_ids_copy(k, s).wait_send()
+        col_copy(k, s).wait_send()
+    for k in range(1, others):
+        block_to_peer(s, lvl_send.at[k], peer(2 * k)).wait_send()
+        block_to_peer(peer(2 * k), fwd_send.at[k], partner).wait_send()
+    block_to_peer(s, lvl_send.at[0], partner).wait_send()
+
+    @pl.when(sends_right | sends_left)
+    def _():
+        lax.fori_loop(0, chunks, lambda k, c: (own_to_lane(k, z).wait_send(), c)[1], 0)
+
+    for i in [0] + early:
+        @pl.when(passes(i))
+        def _(i=i):
+            lax.fori_loop(0, chunks, lambda k, c: (passed_on(i, k, z).wait_send(), c)[1], 0)
+
+        @pl.when(visits(i))
+        def _(i=i):
+            ret_copy(i, z, i).wait_send()
+
+
+def by_meeting(embeddings, cluster_ids, chunks):
+    rows, features = embeddings.shape
+    groups = lax.axis_size("grp")
+    subgroup = lax.axis_size("sub")
+    dma = pltpu.SemaphoreType.DMA
+    best = pl.pallas_call(
+        functools.partial(meet_kernel, groups, subgroup, chunks),
+        out_shape=jax.ShapeDtypeStruct((1, rows), jnp.float32),
+        in_specs=[pl.BlockSpec(memory_space=pltpu.VMEM)] * 2,
+        out_specs=pl.BlockSpec(memory_space=pltpu.VMEM),
+        scratch_shapes=[
+            pltpu.VMEM((subgroup * rows, features), jnp.bfloat16),
+            pltpu.VMEM((groups, rows, features), jnp.bfloat16),
+            pltpu.VMEM((groups, 1, rows), jnp.int32),
+            pltpu.VMEM((subgroup, 1, rows), jnp.int32),
+            pltpu.VMEM((groups, rows, LANES), jnp.int32),
+            pltpu.VMEM((groups, rows, LANES), jnp.float32),
+            pltpu.VMEM((SUBLANES, subgroup * rows), jnp.float32),
+            pltpu.VMEM((groups, 1, rows), jnp.float32),
+            pltpu.VMEM((groups, 1, rows), jnp.float32),
+            pltpu.VMEM((subgroup, 1, rows), jnp.float32),
+            pltpu.VMEM((subgroup, 1, rows), jnp.float32),
+            dma((groups,)), dma((groups,)),
+            dma((subgroup,)), dma((subgroup,)),
+            dma((subgroup,)), dma((subgroup,)), dma((subgroup,)),
+            dma((groups, chunks)), dma((groups, chunks)),
+            dma((groups,)), dma((groups,)),
+            dma((subgroup,)), dma((subgroup,)),
+        ],
+        compiler_params=pltpu.CompilerParams(collective_id=0, has_side_effects=True),
+    )(embeddings, cluster_ids.reshape(1, rows))
+    return best.reshape(rows)
+
+
+def local(embeddings, cluster_ids):
+    rows, features = embeddings.shape
+    groups = lax.axis_size("grp")
+    subgroup = lax.axis_size("sub")
+    held = (groups + subgroup) * rows * features * embeddings.dtype.itemsize
+    chunks = max(1, rows // 64)
+    if held <= VMEM_BUDGET and subgroup % 2 == 0 and groups > 2 and rows % (LANES * 2) == 0:
+        return by_meeting(embeddings, cluster_ids, chunks)
+    return by_owner(embeddings, cluster_ids)
+
+
 def solution(mesh):
     return jax.shard_map(
         local,

time: 87.1 us -> 43.3 us (0.50)
  Pallas kernels: 0 us -> 41.9 us
  blocking collectives: 40 us -> 0 us
  waiting for transfers between devices: 27 us -> 0 us
  starting transfers between devices: 7.18 us -> 0 us
  other arithmetic: 5.22 us -> 0 us
  local copies, waits for them, and re-layouts: 4.86 us -> 1.22 us
  matrix products: 2.44 us -> 0 us
    pallas_call x0 -> x1, Pallas kernels: none -> 41.9 us  [by_meeting(): pl.pallas_call(functools.partial(meet_kernel, groups, subgroup, chunks),...]
    all_to_all x2 -> x0, blocking collectives: 40 us -> none  [the longest x1 31.9 us: local(): lax.all_to_all(outgoing.reshape(groups, capacity, features), 'grp', split...]
    ppermute x5 -> x0, waiting for transfers between devices: 21.6 us -> none  [from_behind(): lax.ppermute(value, axis, [(i, (i + by) % peers) for i in range(peers)])]
    all_to_all x1 -> x0, waiting for transfers between devices: 5.37 us -> none  [local(): lax.all_to_all(highest.reshape(groups, capacity), 'grp', split_axis=0, co...]
    ppermute x5 -> x0, starting transfers between devices: 3.93 us -> none  [from_behind(): lax.ppermute(value, axis, [(i, (i + by) % peers) for i in range(peers)])]
    all_to_all x1 -> x0, starting transfers between devices: 3.24 us -> none  [local(): lax.all_to_all(highest.reshape(groups, capacity), 'grp', split_axis=0, co...]
    gather x1 -> x0, local copies, waits for them, and re-layouts: 2.5 us -> none  [local(): return returned.reshape(groups * capacity)[slot_index]]
    dot_general x3 -> x0, matrix products: 2.44 us -> none  [masked_maxima(): jnp.dot(left_rows, right_rows.T, preferred_element_type=jnp.float32)]
  transfers between devices with their start and end apart: 6 -> 0, of which waited for: 4 -> 0; matrix products, arithmetic and copies ran while one was open for 4% -> 0% of each run, Pallas kernels for 0% -> 0%
where the time goes in v1:
time: 43.3 us; the launch traced here: 43.2 us
  Pallas kernels  41.9 us (97%)
  local copies, waits for them, and re-layouts  1.22 us (3%)
    pallas_call x1, Pallas kernels, by_meeting(): pl.pallas_call(functools.partial(meet_kernel, groups, subgroup, chunks),...  41.9 us
    unnamed x3, local copies, waits for them, and re-layouts  1.22 us

profile of v1, /device:TPU:0, one launch (start us, length us, event | category | flops | bytes accessed | tf_op | source)
XLA Modules:
  0.0 43.2 jit_solution(1257868996739360083)
XLA Ops:
  0.0 41.9 %shard_map.28 = f32[1,256]{1,0:T(1,128)} custom-call(bf16[256,1024]{1,0:T(8,128)(2,1)} %emb_ref.1, s32[1,256]{1,0:T(1,128)} %bitcast.3), custom_call_target="tpu_custom_call" | custom-call | tf_op jit(solution)/shard_map/pallas_call | solution.py:328
  41.9 0.0 copy-start
  41.9 0.7 %copy-done = f32[1,256]{1,0:T(1,128)S(1)} copy-done((f32[1,256]{1,0:T(1,128)S(1)}, f32[1,256]{1,0:T(1,128)}, u32[]{:S(2)}) %copy-start) | copy-done | bytes 1048
  42.6 0.6 %copy.4 = f32[256]{0:T(256)} copy(f32[256]{0:T(256)S(1)} %bitcast.2) | data formatting | bytes 2048
Async XLA Ops:
  41.9 0.7 %copy-start = (f32[1,256]{1,0:T(1,128)S(1)}, f32[1,256]{1,0:T(1,128)}, u32[]{:S(2)}) copy-start(f32[1,256]{1,0:T(1,128)} %shard_map.28) | copy-start | bytes 3076

commit v2 on v1

--- a/solution.py
+++ b/solution.py
@@ -87,18 +87,24 @@
 def meet_kernel(
     groups, subgroup, chunks,
     emb_ref, ids_ref, out_ref,
-    level, foreign, lane_ids, level_ids, ids_col, row_part, col_part,
+    level, foreign, relay, lane_ids, level_ids, ids_col, row_part, col_part,
     ret_out, ret_in, col_out, col_in,
     ids_send, ids_recv, lid_send, lid_recv, lvl_send, lvl_recv, fwd_send,
-    z_send, z_recv, ret_send, ret_recv, col_send, col_recv,
+    z_send, z_recv, out_send, relay_send, relay_recv, ret_send, ret_recv, col_send, col_recv,
 ):
     rows, features = emb_ref.shape
     size = rows // chunks
     pivot = groups // 2
-    z = lax.axis_index("grp")
+    rep = lax.axis_index("rep")
+    depth = lax.axis_index("grp")
+    z = depth * (1 - rep) + (groups - 1 - depth) * rep
     s = lax.axis_index("sub")
     partner = s + 1 - 2 * lax.rem(s, 2)
     others = subgroup // 2
+    odd = lax.rem(s, 2) == 1
+    even = lax.rem(s, 2) == 0
+    relay_at = groups - 1 - z
+    across_y = {"rep": 1 - rep}
 
     def peer(k):
         return lax.rem(s + k, subgroup)
@@ -106,11 +112,16 @@
     def lane(k):
         return lax.rem(z + k, groups)
 
+    def at(where):
+        return {"grp": where * (1 - rep) + (groups - 1 - where) * rep}
+
     barrier = pltpu.get_barrier_semaphore()
     for k in range(1, subgroup):
         pl.semaphore_signal(barrier, 1, device_id={"sub": peer(k)}, device_id_type=MESH)
     for k in range(1, groups):
-        pl.semaphore_signal(barrier, 1, device_id={"grp": lane(k)}, device_id_type=MESH)
+        pl.semaphore_signal(barrier, 1, device_id=at(lane(k)), device_id_type=MESH)
+
+    pl.semaphore_signal(barrier, 1, device_id=across_y, device_id_type=MESH)
 
     def slot(b):
         return pl.ds(pl.multiple_of(b * rows, rows), rows)
@@ -129,7 +140,7 @@
     level_ids[s] = ids_ref[...]
     lane_ids[z] = ids_ref[...]
     col_part[...] = jnp.full(col_part.shape, -1.0, jnp.float32)
-    pl.semaphore_wait(barrier, subgroup + groups - 2)
+    pl.semaphore_wait(barrier, subgroup + groups - 1)
 
     def remote(src, dst, send, recv, where):
         return pltpu.make_async_remote_copy(
@@ -141,17 +152,39 @@
         return remote(ids_ref, level_ids.at[owner], lid_send.at[k], lid_recv.at[owner], {"sub": peer(k)})
 
     def lane_ids_copy(k, owner):
-        return remote(ids_ref, lane_ids.at[owner], ids_send.at[k], ids_recv.at[owner], {"grp": lane(k)})
+        return remote(ids_ref, lane_ids.at[owner], ids_send.at[k], ids_recv.at[owner], at(lane(k)))
 
     def own_to_lane(k, where):
         return remote(
             level.at[piece(s, k), :], foreign.at[z, part(k), :], z_send.at[z, k], z_recv.at[z, k],
-            {"grp": where},
+            at(where),
         )
 
     def passed_on(i, k, where):
         block = foreign.at[i, part(k), :]
-        return remote(block, block, z_send.at[i, k], z_recv.at[i, k], {"grp": where})
+        return remote(block, block, z_send.at[i, k], z_recv.at[i, k], at(where))
+
+    def own_across(k):
+        return remote(
+            level.at[piece(s, k), :], relay.at[z, part(k), :], out_send.at[k], relay_recv.at[z, k],
+            across_y,
+        )
+
+    def relayed(i, k):
+        block = relay.at[i, part(k), :]
+        return remote(block, block, relay_send.at[i, k], relay_recv.at[i, k], at(z - 1))
+
+    def passed_across(i, k):
+        return remote(
+            foreign.at[i, part(k), :], relay.at[i, part(k), :], z_send.at[i, k], relay_recv.at[i, k],
+            across_y,
+        )
+
+    def back_across(i, k):
+        return remote(
+            relay.at[i, part(k), :], foreign.at[i, part(k), :], relay_send.at[i, k], z_recv.at[i, k],
+            across_y,
+        )
 
     def block_to_peer(owner, send, where):
         block = level.at[slot(owner), :]
@@ -162,8 +195,13 @@
     for k in range(1, subgroup):
         level_ids_copy(k, s).start()
 
-    sends_right = z < pivot
+    at_bank = odd & (z == pivot - 1)
+    sends_right = (z < pivot) & (even | (z < pivot - 1))
     sends_left = z > pivot
+
+    @pl.when(at_bank)
+    def _():
+        lax.fori_loop(0, chunks, lambda k, c: (own_across(k).start(), c)[1], 0)
 
     @pl.when(sends_right)
     def _():
@@ -180,25 +218,86 @@
     def visits(i):
         return z > i if i < pivot else (z >= pivot) & (z < i)
 
+    turned = lax.rem(s, 2) * (z // (pivot + 1))
+
     def passes(i):
-        return (z > i) & (z < groups - 1) if i < pivot else (z > pivot) & (z < i)
+        if i >= pivot:
+            return (z > pivot) & (z < i)
+        if i % 2 == 0:
+            return (z > i) & (z < groups - 1) & (even | (z < pivot - 1) | (z > pivot - 1))
+        return (z > i) & ((even & (z < groups - 1)) | (odd & ((z < pivot - 1) | (z > pivot))))
 
     def onward(i):
-        return z + 1 if i < pivot else z - 1
-
-    def take(i, k):
-        passed_on(i, k, z).wait_recv()
-
-        @pl.when(passes(i))
+        if i >= pivot:
+            return z - 1
+        return z + 1 if i % 2 == 0 else z + 1 - 2 * turned
+
+    def take(i):
+        def one(k, carry):
+            passed_on(i, k, z).wait_recv()
+
+            @pl.when(passes(i))
+            def _():
+                passed_on(i, k, onward(i)).start()
+
+            return carry
+
+        lax.fori_loop(0, chunks, one, 0)
+
+    last_stop = [pivot if i % 2 == 0 else groups - 1 for i in range(pivot)]
+
+    def relays(i):
+        return odd & (relay_at >= pivot - 1) & (relay_at <= last_stop[i])
+
+    def relay_on(i, k):
+        @pl.when(relays(i))
         def _():
-            passed_on(i, k, onward(i)).start()
-
-    early = list(range(pivot - 1, 0, -1)) + list(range(pivot + 1, groups))
-    for i in early + [0]:
-        @pl.when(visits(i) if i else z == 1)
-        def _(i=i):
-            lax.fori_loop(0, chunks, lambda k, c: (take(i, k), c)[1], 0)
-
+            relayed(i, k).wait_recv()
+
+            @pl.when(relay_at < last_stop[i])
+            def _():
+                relayed(i, k).start()
+
+            @pl.when(relay_at == last_stop[i])
+            def _():
+                back_across(i, k).start()
+
+    for i in range(pivot - 1, -1, -1):
+        def relay_step(k, carry, i=i):
+            relay_on(i, k)
+            if i > 0:
+                @pl.when(at_bank)
+                def _():
+                    passed_on(i - 1, k, z).wait_recv()
+                    passed_across(i - 1, k).start()
+
+            return carry
+
+        @pl.when(odd)
+        def _(relay_step=relay_step):
+            lax.fori_loop(0, chunks, relay_step, 0)
+
+    def soon(i):
+        if i >= pivot:
+            return visits(i)
+        if i % 2 == 0:
+            return visits(i) & (z <= pivot)
+        return visits(i) & (even | (z < pivot) | (z == groups - 1))
+
+    def later(i):
+        if i % 2 == 0:
+            return z > pivot
+        return odd & (z >= pivot) & (z < groups - 1)
+
+    sources = list(range(pivot - 1, -1, -1)) + list(range(pivot + 1, groups))
+
+    def take_soon(mine):
+        for i in sources:
+            @pl.when(soon(i) & mine & (even | (z < pivot - 1) | (z > pivot - 1)) if i < pivot else soon(i) & mine)
+            def _(i=i):
+                take(i)
+
+    take_soon(even)
     for k in range(1, others):
         came_from = peer(2 * k)
         block_to_peer(came_from, lvl_send.at[0], s).wait_recv()
@@ -207,6 +306,7 @@
         came_from = lax.rem(partner + 2 * k, subgroup)
         block_to_peer(came_from, lvl_send.at[0], s).wait_recv()
 
+    take_soon(odd)
     for k in range(1, groups):
         lane_ids_copy(k, lane(k)).wait_recv()
     for k in range(1, subgroup):
@@ -216,70 +316,54 @@
 
     width = subgroup * rows
 
-    def meet(lines, own_ids, shift, store_row, keep_columns):
+    def meet(block, i, own):
         similar = lax.dot_general(
-            lines, level[...], (((1,), (1,)), ((), ())), preferred_element_type=jnp.float32
-        )
-        best = jnp.full((size, LANES), -1.0, jnp.float32)
-        for at in range(0, width, LANES):
-            ids_at = level_ids[at // rows, :, at % rows : at % rows + LANES]
-            same = own_ids == ids_at
-            if shift is not None:
-                across = lax.broadcasted_iota(jnp.int32, (size, LANES), 1) + at
-                down = lax.broadcasted_iota(jnp.int32, (size, LANES), 0) + shift
+            block, level[...], (((1,), (1,)), ((), ())), preferred_element_type=jnp.float32
+        )
+        own_ids = ids_col[i]
+        best = jnp.full((rows, LANES), -1.0, jnp.float32)
+        for col in range(0, width, LANES):
+            same = own_ids == level_ids[col // rows, :, col % rows : col % rows + LANES]
+            if own:
+                across = lax.broadcasted_iota(jnp.int32, (rows, LANES), 1) + col
+                down = lax.broadcasted_iota(jnp.int32, (rows, LANES), 0) + s * rows
                 same = same & (across != down)
-            kept = jnp.where(same, similar[:, at : at + LANES], jnp.float32(-1.0))
+            kept = jnp.where(same, similar[:, col : col + LANES], jnp.float32(-1.0))
             best = jnp.maximum(best, kept)
-            if keep_columns:
-                columns = jnp.max(kept.reshape(size // SUBLANES, SUBLANES, LANES), axis=0)
-                col_part[:, at : at + LANES] = jnp.maximum(col_part[:, at : at + LANES], columns)
-        store_row(best)
-
-    def meet_foreign(i, k):
-        def store(best):
-            row_part[i, part(k), :] = best
-
-        meet(foreign[i, part(k), :], ids_col[i, part(k), :], None, store, True)
-
-    def step(k, carry):
-        def store(best):
-            row_part[z, part(k), :] = best
-
-        meet(level[piece(s, k), :], ids_col[z, part(k), :], s * rows + k * size, store, False)
-        for i in early:
-            @pl.when(visits(i))
-            def _(i=i):
-                meet_foreign(i, k)
-
-        @pl.when(z > 1)
-        def _():
-            take(0, k)
-
-        @pl.when(z > 0)
-        def _():
-            meet_foreign(0, k)
-
-        return carry
-
-    lax.fori_loop(0, chunks, step, 0)
+            if not own:
+                columns = jnp.max(kept.reshape(rows // SUBLANES, SUBLANES, LANES), axis=0)
+                col_part[:, col : col + LANES] = jnp.maximum(col_part[:, col : col + LANES], columns)
+        row_part[i] = best
+
+    meet(level[slot(s), :], z, True)
+    for i in sources:
+        @pl.when(soon(i))
+        def _(i=i):
+            meet(foreign[i], i, False)
+
+    for i in range(pivot):
+        @pl.when(later(i))
+        def _(i=i):
+            take(i)
+            meet(foreign[i], i, False)
 
     def flat(i):
         return jnp.max(row_part[i].T, axis=0, keepdims=True)
 
     def ret_copy(i, owner, where):
-        return remote(ret_out.at[i], ret_in.at[owner], ret_send.at[i], ret_recv.at[owner], {"grp": where})
+        return remote(ret_out.at[i], ret_in.at[owner], ret_send.at[i], ret_recv.at[owner], at(where))
 
     def col_copy(k, owner):
         return remote(col_out.at[peer(k)], col_in.at[owner], col_send.at[k], col_recv.at[owner], {"sub": peer(k)})
 
-    for i in [0] + early:
+    for i in sources:
         @pl.when(visits(i))
         def _(i=i):
             ret_out[i] = flat(i)
 
     for b in range(subgroup):
         col_out[b] = jnp.max(col_part[:, b * rows : (b + 1) * rows], axis=0, keepdims=True)
-    for i in [0] + early:
+    for i in sources:
         @pl.when(visits(i))
         def _(i=i):
             ret_copy(i, z, i).start()
@@ -306,14 +390,28 @@
         block_to_peer(peer(2 * k), fwd_send.at[k], partner).wait_send()
     block_to_peer(s, lvl_send.at[0], partner).wait_send()
 
+    @pl.when(at_bank)
+    def _():
+        lax.fori_loop(0, chunks, lambda k, c: (own_across(k).wait_send(), c)[1], 0)
+
+    for i in range(pivot):
+        @pl.when(relays(i))
+        def _(i=i):
+            lax.fori_loop(0, chunks, lambda k, c: (relayed(i, k).wait_send(), c)[1], 0)
+
     @pl.when(sends_right | sends_left)
     def _():
         lax.fori_loop(0, chunks, lambda k, c: (own_to_lane(k, z).wait_send(), c)[1], 0)
 
-    for i in [0] + early:
+    for i in sources:
         @pl.when(passes(i))
         def _(i=i):
             lax.fori_loop(0, chunks, lambda k, c: (passed_on(i, k, z).wait_send(), c)[1], 0)
+
+        if i < pivot - 1:
+            @pl.when(at_bank)
+            def _(i=i):
+                lax.fori_loop(0, chunks, lambda k, c: (passed_across(i, k).wait_send(), c)[1], 0)
 
         @pl.when(visits(i))
         def _(i=i):
@@ -333,6 +431,7 @@
         scratch_shapes=[
             pltpu.VMEM((subgroup * rows, features), jnp.bfloat16),
             pltpu.VMEM((groups, rows, features), jnp.bfloat16),
+            pltpu.VMEM((groups // 2, rows, features), jnp.bfloat16),
             pltpu.VMEM((groups, 1, rows), jnp.int32),
             pltpu.VMEM((subgroup, 1, rows), jnp.int32),
             pltpu.VMEM((groups, rows, LANES), jnp.int32),
@@ -346,6 +445,7 @@
             dma((subgroup,)), dma((subgroup,)),
             dma((subgroup,)), dma((subgroup,)), dma((subgroup,)),
             dma((groups, chunks)), dma((groups, chunks)),
+            dma((chunks,)), dma((groups // 2, chunks)), dma((groups // 2, chunks)),
             dma((groups,)), dma((groups,)),
             dma((subgroup,)), dma((subgroup,)),
         ],
@@ -359,8 +459,9 @@
     groups = lax.axis_size("grp")
     subgroup = lax.axis_size("sub")
     held = (groups + subgroup) * rows * features * embeddings.dtype.itemsize
-    chunks = max(1, rows // 64)
-    if held <= VMEM_BUDGET and subgroup % 2 == 0 and groups > 2 and rows % (LANES * 2) == 0:
+    chunks = max(1, rows // 32)
+    paired = lax.axis_size("rep") == 2 and subgroup % 2 == 0 and groups // 2 == 2
+    if held <= VMEM_BUDGET and paired and groups % 2 == 0 and rows % (LANES * 2) == 0:
         return by_meeting(embeddings, cluster_ids, chunks)
     return by_owner(embeddings, cluster_ids)
 

time: 43.3 us -> 37.9 us (0.88)
  the two profiles are of different devices: /device:TPU:0 before, /device:TPU:1 now
where the time goes in v2:
time: 37.9 us; the launch traced here: 37.8 us
  Pallas kernels  36.5 us (96%)
  local copies, waits for them, and re-layouts  1.22 us (3%)
    pallas_call x1, Pallas kernels, by_meeting(): pl.pallas_call(functools.partial(meet_kernel, groups, subgroup, chunks),...  36.5 us
    unnamed x3, local copies, waits for them, and re-layouts  1.22 us

profile of v2, /device:TPU:1, one launch (start us, length us, event | category | flops | bytes accessed | tf_op | source)
XLA Modules:
  0.0 37.8 jit_solution(3005204708452700887)
XLA Ops:
  0.0 36.5 %shard_map.28 = f32[1,256]{1,0:T(1,128)} custom-call(bf16[256,1024]{1,0:T(8,128)(2,1)} %emb_ref.1, s32[1,256]{1,0:T(1,128)} %bitcast.3), custom_call_target="tpu_custom_call" | custom-call | tf_op jit(solution)/shard_map/pallas_call | solution.py:426
  36.5 0.0 copy-start
  36.5 0.7 %copy-done = f32[1,256]{1,0:T(1,128)S(1)} copy-done((f32[1,256]{1,0:T(1,128)S(1)}, f32[1,256]{1,0:T(1,128)}, u32[]{:S(2)}) %copy-start) | copy-done | bytes 1048
  37.2 0.6 %copy.4 = f32[256]{0:T(256)} copy(f32[256]{0:T(256)S(1)} %bitcast.2) | data formatting | bytes 2048
Async XLA Ops:
  36.5 0.7 %copy-start = (f32[1,256]{1,0:T(1,128)S(1)}, f32[1,256]{1,0:T(1,128)}, u32[]{:S(2)}) copy-start(f32[1,256]{1,0:T(1,128)} %shard_map.28) | copy-start | bytes 3076

commit v3 on v2

--- a/solution.py
+++ b/solution.py
@@ -232,18 +232,18 @@
             return z - 1
         return z + 1 if i % 2 == 0 else z + 1 - 2 * turned
 
-    def take(i):
-        def one(k, carry):
-            passed_on(i, k, z).wait_recv()
-
-            @pl.when(passes(i))
-            def _():
-                passed_on(i, k, onward(i)).start()
-
-            return carry
-
-        lax.fori_loop(0, chunks, one, 0)
-
+    def take_one(i, k):
+        passed_on(i, k, z).wait_recv()
+
+        @pl.when(passes(i))
+        def _():
+            passed_on(i, k, onward(i)).start()
+
+    def take(i, first=0):
+        lax.fori_loop(first, chunks, lambda k, c: (take_one(i, k), c)[1], 0)
+
+    lag = chunks // 2
+    lagged = odd & (z == pivot)
     last_stop = [pivot if i % 2 == 0 else groups - 1 for i in range(pivot)]
 
     def relays(i):
@@ -271,11 +271,20 @@
                     passed_on(i - 1, k, z).wait_recv()
                     passed_across(i - 1, k).start()
 
+            else:
+                @pl.when(lagged & (k >= lag))
+                def _():
+                    take_one(0, k - lag)
+
             return carry
 
         @pl.when(odd)
         def _(relay_step=relay_step):
             lax.fori_loop(0, chunks, relay_step, 0)
+
+    @pl.when(lagged)
+    def _():
+        take(0, chunks - lag)
 
     def soon(i):
         if i >= pivot:
@@ -293,7 +302,7 @@
 
     def take_soon(mine):
         for i in sources:
-            @pl.when(soon(i) & mine & (even | (z < pivot - 1) | (z > pivot - 1)) if i < pivot else soon(i) & mine)
+            @pl.when(soon(i) & mine & (even | (z < pivot) | (z > pivot) if i == 0 else z >= 0) & (even | (z < pivot - 1) | (z > pivot - 1)) if i < pivot else soon(i) & mine)
             def _(i=i):
                 take(i)
 
@@ -335,38 +344,34 @@
                 col_part[:, col : col + LANES] = jnp.maximum(col_part[:, col : col + LANES], columns)
         row_part[i] = best
 
+    def flat(i):
+        return jnp.max(row_part[i].T, axis=0, keepdims=True)
+
+    def ret_copy(i, owner, where):
+        return remote(ret_out.at[i], ret_in.at[owner], ret_send.at[i], ret_recv.at[owner], at(where))
+
+    def give_back(i):
+        meet(foreign[i], i, False)
+        ret_out[i] = flat(i)
+        ret_copy(i, z, i).start()
+
     meet(level[slot(s), :], z, True)
     for i in sources:
         @pl.when(soon(i))
         def _(i=i):
-            meet(foreign[i], i, False)
+            give_back(i)
 
     for i in range(pivot):
         @pl.when(later(i))
         def _(i=i):
             take(i)
-            meet(foreign[i], i, False)
-
-    def flat(i):
-        return jnp.max(row_part[i].T, axis=0, keepdims=True)
-
-    def ret_copy(i, owner, where):
-        return remote(ret_out.at[i], ret_in.at[owner], ret_send.at[i], ret_recv.at[owner], at(where))
+            give_back(i)
 
     def col_copy(k, owner):
         return remote(col_out.at[peer(k)], col_in.at[owner], col_send.at[k], col_recv.at[owner], {"sub": peer(k)})
 
-    for i in sources:
-        @pl.when(visits(i))
-        def _(i=i):
-            ret_out[i] = flat(i)
-
     for b in range(subgroup):
         col_out[b] = jnp.max(col_part[:, b * rows : (b + 1) * rows], axis=0, keepdims=True)
-    for i in sources:
-        @pl.when(visits(i))
-        def _(i=i):
-            ret_copy(i, z, i).start()
     for k in range(1, subgroup):
         col_copy(k, s).start()
 

time: 37.9 us -> 37.9 us (level)
  the two profiles are of different devices: /device:TPU:1 before, /device:TPU:0 now
where the time goes in v3:
time: 37.9 us; the launch traced here: 37.8 us
  Pallas kernels  36.5 us (96%)
  local copies, waits for them, and re-layouts  1.22 us (3%)
    pallas_call x1, Pallas kernels, by_meeting(): pl.pallas_call(functools.partial(meet_kernel, groups, subgroup, chunks),...  36.5 us
    unnamed x3, local copies, waits for them, and re-layouts  1.22 us

profile of v3, /device:TPU:0, one launch (start us, length us, event | category | flops | bytes accessed | tf_op | source)
XLA Modules:
  0.0 37.8 jit_solution(1356110387059133560)
XLA Ops:
  0.0 36.5 %shard_map.28 = f32[1,256]{1,0:T(1,128)} custom-call(bf16[256,1024]{1,0:T(8,128)(2,1)} %emb_ref.1, s32[1,256]{1,0:T(1,128)} %bitcast.3), custom_call_target="tpu_custom_call" | custom-call | tf_op jit(solution)/shard_map/pallas_call | solution.py:431
  36.5 0.0 copy-start
  36.5 0.7 %copy-done = f32[1,256]{1,0:T(1,128)S(1)} copy-done((f32[1,256]{1,0:T(1,128)S(1)}, f32[1,256]{1,0:T(1,128)}, u32[]{:S(2)}) %copy-start) | copy-done | bytes 1048
  37.2 0.6 %copy.4 = f32[256]{0:T(256)} copy(f32[256]{0:T(256)S(1)} %bitcast.2) | data formatting | bytes 2048
Async XLA Ops:
  36.5 0.7 %copy-start = (f32[1,256]{1,0:T(1,128)S(1)}, f32[1,256]{1,0:T(1,128)}, u32[]{:S(2)}) copy-start(f32[1,256]{1,0:T(1,128)} %shard_map.28) | copy-start | bytes 3076
